TPU v7x, 32 devices: a whole 2x2x4 slice. The times are simulated.
32 devices in a mesh: ctx: 16 (over z, x, core), head: 2 (over y).
Axes of the slice: x: 2, y: 2, z: 4, core: 2. Of those that a mesh axis runs over, the one named last changes fastest.
Arguments:
- query_rows: bfloat16 [8192, 2048], P('ctx', 'head'), may hold values from -60 to 60
- key_rows: bfloat16 [8192, 2048], P('ctx', 'head'), may hold values from -6 to 6
- value_rows: bfloat16 [8192, 2048], P('ctx', 'head'), may hold values from -60 to 60
- log_gate: float32 [16, 8192], P('head', 'ctx'), may hold values from -0.5 to 0
- conv_weight: float32 [3, 4, 2048], P(None, None, 'head'), may hold values from -3 to 3
- norm_gain: float32 [2048], P('head'), may hold values from 0.5 to 1.5
- mixed_grad: bfloat16 [8192, 2048], P('ctx', 'head'), may hold values from -24 to 24
Outputs:
- mixer_out: bfloat16 [8192, 2048], P('ctx', 'head')
- query_grad: bfloat16 [8192, 2048], P('ctx', 'head')
- key_grad: bfloat16 [8192, 2048], P('ctx', 'head')
- value_grad: bfloat16 [8192, 2048], P('ctx', 'head')
- conv_grad: float32 [3, 4, 2048], P(None, None, 'head')
- gain_grad: float32 [2048], P('head')
All inputs are finite; a program needn't handle non-finite values.
Results may differ from a plain program's by a relative error of at most 0.015.
Values may be sent and summed in bfloat16 or wider, within the bound.
A program may use at most 128 MiB of HBM per device.

v0:
```python
import jax
import jax.numpy as jnp
from jax import lax
from jax.sharding import PartitionSpec as P

HD = 128
TAPS = 4
GROUP = 512
D = 2048
norm_epsilon = 1e-05


def shifted(block, axis, distance):
    devices = range(lax.axis_size(axis))
    route = [(i - distance, i) for i in devices if i - distance in devices]
    return lax.ppermute(block, axis, route)


def prefix(value, axis, join, neutral):
    count = lax.axis_size(axis)
    place = lax.axis_index(axis)
    ahead = count - 1 - place
    gathered = jax.tree.map(
        lambda a, kind: lax.all_gather(a.astype(kind), axis), value, (jnp.bfloat16, jnp.bfloat16)
    )
    state = jax.tree.map(lambda a, e: jnp.zeros_like(a) + jnp.asarray(e, a.dtype), value, neutral)

    def one(turn, state):
        source = count - 1 - turn
        return join(
            state,
            jax.tree.map(
                lambda a, own: lax.dynamic_index_in_dim(a, source, 0, False).astype(own.dtype),
                gathered,
                value,
            ),
        )

    return lax.fori_loop(0, ahead, one, state)


def rounded(values):
    return values.astype(jnp.bfloat16)


def decay_tables(gate_blocks):
    running = jnp.cumsum(gate_blocks, axis=-1)
    closing = running[..., -1]
    gap_matrix = running[..., :, None] - running[..., None, :]
    block_size = gate_blocks.shape[-1]
    lower_mask = jnp.arange(block_size)[:, None] >= jnp.arange(block_size)[None, :]
    weights = jnp.where(lower_mask, jnp.exp(jnp.minimum(gap_matrix, 0.0)), 0.0)
    return (running, closing, weights)


def chain_step(earlier, later_part):
    return (
        earlier[0] + later_part[0],
        jnp.exp(later_part[0])[..., None, None] * earlier[1] + later_part[1],
    )


def local_chain(closing, blocks, backwards):

    def advance(partial_sum, block_item):
        return (chain_step(partial_sum, block_item), partial_sum)

    initial = (jnp.zeros(closing.shape[1:], jnp.float32), jnp.zeros(blocks.shape[1:], jnp.float32))
    return lax.scan(advance, initial, (closing, blocks), reverse=backwards)


def conv_forward(rim_rows, rows, weight, tok_here):
    extended = jnp.concatenate([rim_rows, rows], axis=0).astype(jnp.float32)
    result = weight[0][None, :] * extended[TAPS - 1 : TAPS - 1 + tok_here]
    for offset in range(1, TAPS):
        result = (
            result
            + weight[offset][None, :] * extended[TAPS - 1 - offset : TAPS - 1 - offset + tok_here]
        )
    return (rounded(result), extended)


def conv_backward(grad_rows, edge_rows, extended, weight, tok_here):
    ahead_all = jnp.concatenate([grad_rows, edge_rows], axis=0)
    input_grad = weight[0][None, :] * grad_rows
    weight_grad = [jnp.sum(grad_rows * extended[TAPS - 1 : TAPS - 1 + tok_here], axis=0)]
    for offset in range(1, TAPS):
        input_grad = input_grad + weight[offset][None, :] * ahead_all[offset : offset + tok_here]
        weight_grad.append(
            jnp.sum(grad_rows * extended[TAPS - 1 - offset : TAPS - 1 - offset + tok_here], axis=0)
        )
    return (rounded(input_grad), jnp.stack(weight_grad))


def body(query_rows, key_rows, value_rows, log_gate, conv_weight, norm_gain, mixed_grad):
    tok_here = query_rows.shape[0]
    width_here = query_rows.shape[1]
    heads_here = width_here // HD
    block_count = tok_here // GROUP
    rim_rows = shifted(
        jnp.stack(
            [
                query_rows[tok_here - (TAPS - 1) :],
                key_rows[tok_here - (TAPS - 1) :],
                value_rows[tok_here - (TAPS - 1) :],
            ]
        ),
        "ctx",
        1,
    )
    query_conv, query_ext = conv_forward(rim_rows[0], query_rows, conv_weight[0], tok_here)
    key_conv, key_ext = conv_forward(rim_rows[1], key_rows, conv_weight[1], tok_here)
    value_conv, value_ext = conv_forward(rim_rows[2], value_rows, conv_weight[2], tok_here)
    query_blocks = query_conv.reshape(block_count, GROUP, heads_here, HD)
    key_blocks = key_conv.reshape(block_count, GROUP, heads_here, HD)
    value_blocks = value_conv.reshape(block_count, GROUP, heads_here, HD)
    gate_blocks = log_gate.reshape(heads_here, block_count, GROUP).transpose(1, 0, 2)
    running, closing, weights = decay_tables(gate_blocks)
    grow_factor = jnp.exp(running).transpose(0, 2, 1)[..., None]
    shrink = jnp.exp(closing[..., None] - running).transpose(0, 2, 1)[..., None]
    scores = jnp.einsum(
        "nthd,nshd->nhts", query_blocks, key_blocks, preferred_element_type=jnp.float32
    )
    weights_low = rounded(scores * weights)
    key_scaled = rounded(key_blocks * shrink)
    blocks = jnp.einsum(
        "nshd,nshe->nhde", key_scaled, value_blocks, preferred_element_type=jnp.float32
    )
    device_sum, before = local_chain(closing, blocks, False)
    zero_state = jnp.zeros((heads_here, HD, HD), jnp.float32)
    all_totals = lax.all_gather(device_sum[0][None], "ctx", axis=0, tiled=True)
    device_index = lax.axis_index("ctx")
    cumulative = jnp.cumsum(all_totals, axis=0)
    before_me = cumulative[device_index] - all_totals[device_index]
    sources = jnp.arange(all_totals.shape[0])
    factor_table = jnp.where(
        (sources < device_index)[:, None],
        jnp.exp(jnp.minimum(before_me[None, :] - cumulative, 0.0)),
        0.0,
    )
    incoming = jnp.einsum(
        "nh,nhde->hde",
        factor_table,
        lax.all_gather(device_sum[1][None], "ctx", axis=0, tiled=True),
        precision=lax.Precision.HIGHEST,
    )
    group_in = jnp.exp(before[0])[..., None, None] * incoming[None] + before[1]
    state_low = rounded(group_in)
    attended = jnp.einsum(
        "nhts,nshe->nthe", weights_low, value_blocks, preferred_element_type=jnp.float32
    )
    attended = (
        attended
        + jnp.einsum("nthd,nhde->nthe", query_blocks, state_low, preferred_element_type=jnp.float32)
        * grow_factor
    )
    attended = attended.reshape(tok_here, width_here)
    grad_wide = mixed_grad.astype(jnp.float32)
    scaled = grad_wide * norm_gain[None, :]
    squares = lax.psum(jnp.sum(attended * attended, axis=1), "head")
    inverse = lax.rsqrt(squares / D + norm_epsilon)
    inner_sum = lax.psum(jnp.sum(scaled * attended, axis=1), "head") / D
    normed = attended * inverse[:, None]
    mixer_out = rounded(normed * norm_gain[None, :])
    gain_part = jnp.sum(grad_wide * normed, axis=0)
    out_grad = rounded(
        inverse[:, None] * (scaled - attended * (inverse * inverse * inner_sum)[:, None])
    )
    grad_blocks = out_grad.reshape(block_count, GROUP, heads_here, HD)
    grad_scores = rounded(
        jnp.einsum("nthe,nshe->nhts", grad_blocks, value_blocks, preferred_element_type=jnp.float32)
        * weights
    )
    query_scaled = rounded(query_blocks * grow_factor)
    back_blocks = jnp.einsum(
        "nthd,nthe->nhde", query_scaled, grad_blocks, preferred_element_type=jnp.float32
    )
    back_sum, back_before = local_chain(closing, back_blocks, True)
    later_state = prefix(
        (back_sum[0], back_sum[1]),
        "ctx",
        chain_step,
        (jnp.zeros((heads_here,), jnp.float32), zero_state),
    )[1]
    later_low = rounded(
        jnp.exp(back_before[0])[..., None, None] * later_state[None] + back_before[1]
    )
    query_cg = jnp.einsum(
        "nhts,nshd->nthd", grad_scores, key_blocks, preferred_element_type=jnp.float32
    )
    query_cg = (
        query_cg
        + jnp.einsum("nthe,nhde->nthd", grad_blocks, state_low, preferred_element_type=jnp.float32)
        * grow_factor
    )
    key_cg = jnp.einsum(
        "nhts,nthd->nshd", grad_scores, query_blocks, preferred_element_type=jnp.float32
    )
    key_cg = (
        key_cg
        + jnp.einsum("nshe,nhde->nshd", value_blocks, later_low, preferred_element_type=jnp.float32)
        * shrink
    )
    value_cg = jnp.einsum(
        "nhts,nthe->nshe", weights_low, grad_blocks, preferred_element_type=jnp.float32
    )
    value_cg = (
        value_cg
        + jnp.einsum("nshd,nhde->nshe", key_blocks, later_low, preferred_element_type=jnp.float32)
        * shrink
    )
    query_cg = query_cg.reshape(tok_here, width_here)
    key_cg = key_cg.reshape(tok_here, width_here)
    value_cg = value_cg.reshape(tok_here, width_here)
    edge_rows = shifted(
        jnp.stack([query_cg[: TAPS - 1], key_cg[: TAPS - 1], value_cg[: TAPS - 1]]), "ctx", -1
    )
    query_grad, query_taps = conv_backward(
        query_cg, edge_rows[0], query_ext, conv_weight[0], tok_here
    )
    key_grad, key_taps = conv_backward(key_cg, edge_rows[1], key_ext, conv_weight[1], tok_here)
    value_grad, value_taps = conv_backward(
        value_cg, edge_rows[2], value_ext, conv_weight[2], tok_here
    )
    conv_part = jnp.stack([query_taps, key_taps, value_taps])
    conv_grad, gain_grad = lax.psum((conv_part, gain_part), "ctx")
    return (mixer_out, query_grad, key_grad, value_grad, conv_grad, gain_grad)


def solution(mesh):
    placed = (
        P("ctx", "head"),
        P("ctx", "head"),
        P("ctx", "head"),
        P("head", "ctx"),
        P(None, None, "head"),
        P("head"),
        P("ctx", "head"),
    )
    return jax.shard_map(
        body,
        mesh=mesh,
        in_specs=placed,
        out_specs=(
            P("ctx", "head"),
            P("ctx", "head"),
            P("ctx", "head"),
            P("ctx", "head"),
            P(None, None, "head"),
            P("head"),
        ),
        check_vma=False,
    )
```

profile of v0, /device:TPU:0, one launch (start us, length us, event | category | flops | bytes accessed | tf_op | source)
XLA Modules:
  0.0 309.8 jit_solution(4000271757423066720)
XLA Ops:
  8.8 2.4 collective-permute-start
  11.2 2.2 reduce-window.6
  16.5 1.7 maximum_convert_fusion
  19.7 1.5 copy.163
  21.2 4.9 %fusion.49 = bf16[64,8,8,128]{3,2,1,0:T(8,128)(2,1)S(1)} fusion(f32[515,1024]{1,0:T(8,128)} %maximum_convert_fusion, f32[1024]{0:T(1024)S(1)} %bitcast.226, f32[1024]{0:T(1024)S(1)} %bitcast.228, f32[1024]{0:T(1024)S(1)} %bitcast.230, f32[1024]{0:T(1024)S(1)} %bitcast.224), kind=kLoop, calls=%fused_computation.94 | loop fusion | flops 4194304 | bytes 9453568
  26.1 1.3 convolution_add_fusion.1
  28.5 22.8 %all-gather = f32[16,8,1]{1,2,0:T(1,128)S(1)} all-gather(f32[1,8,1]{1,2,0:T(1,128)S(1)} %get-tuple-element.187), channel_id=2, replica_groups=mesh['ctx'=16,'head'=2] {'ctx'}, dimensions={0}, use_global_device_ids=true | all-gather | bytes 544 | tf_op jit(solution)/shard_map/all_gather | solution.py:131
  52.4 1.4 bitcast_add_fusion
  53.7 1.5 maximum_convert_fusion.1
  55.3 1.3 copy-done
  56.6 1.9 add_convert_fusion.1
  58.5 2.3 copy.213
  62.0 2.9 multiply_convert_fusion.1
  65.0 2.0 copy-done.2
  66.9 2.8 fusion.42
  69.8 35.3 %all-gather.7.cloned.1.call-done = f32[128,128,128]{2,1,0:T(8,128)} async-done(((f32[8,128,128]{2,1,0:T(8,128)}), f32[128,128,128]{2,1,0:T(8,128)}) %all-gather.7.cloned.1.call-update) | async-done | bytes 8388624 | tf_op jit(solution)/shard_map/all_gather | solution.py:144
  105.1 12.5 %fusion = f32[8,1,128,128]{3,1,2,0:T(1,128)S(1)} fusion(f32[16,8,1,1]{0,2,3,1:T(1,128)S(1)} %copy.206, f32[16,8,128,128]{3,2,1,0:T(8,128)} %bitcast.188), kind=kOutput, calls=%fused_computation.2 | convolution fusion | flops 25165824 | bytes 8913408 | tf_op jit(solution)/shard_map/nh,nhde->hde/dot_general | solution.py:141
  117.6 1.9 multiply_reduce_fusion.12
  119.5 5.1 %psum.28 = f32[512]{0:T(512)S(1)} all-reduce(f32[512]{0:T(512)S(1)} %get-tuple-element.206), channel_id=1, replica_groups=mesh['ctx'=16,'head'=2] {'head'}, use_global_device_ids=true, to_apply=%region_4.5 | all-reduce | flops 512 | bytes 4096 | tf_op jit(solution)/shard_map/psum | solution.py:160
  124.7 2.9 copy.169
  127.6 2.6 fusion.7
  130.2 4.9 %psum.29 = f32[512]{0:T(512)S(1)} all-reduce(f32[512]{0:T(512)S(1)} %get-tuple-element.166), channel_id=1, replica_groups=mesh['ctx'=16,'head'=2] {'head'}, use_global_device_ids=true, to_apply=%region_6.7 | all-reduce | flops 512 | bytes 4096 | tf_op jit(solution)/shard_map/psum | solution.py:162
  135.2 3.9 %fusion.6 = (bf16[512,1024]{1,0:T(8,128)(2,1)}, bf16[512,1024]{1,0:T(8,128)(2,1)}) fusion(bf16[512,1024]{1,0:T(8,128)(2,1)} %param.15, f32[512,1024]{1,0:T(8,128)} %copy.169, f32[512]{0:T(512)S(1)} %multiply_multiply_fusion, f32[1024]{0:T(1024)S(1)} %copy-done.25, f32[512]{0:T(512)S(1)} %add_rsqrt_fusion), kind=kLoop, calls=%fused_computation.19 | loop fusion | flops 4718592 | bytes 5251072 | tf_op jit(solution)/shard_map/convert_element_type | solution.py:43
  139.0 2.3 copy.214
  141.3 2.7 fusion.39
  144.0 18.6 %all-gather.3 = bf16[16,8,1]{1,2,0:T(2,128)(2,1)S(1)} all-gather(bf16[1,8,1]{1,2,0:T(2,128)(2,1)S(1)} %slice.396), channel_id=5, replica_groups=mesh['ctx'=16,'head'=2] {'ctx'}, dimensions={0}, use_global_device_ids=true | all-gather | bytes 272 | tf_op jit(solution)/shard_map/all_gather | solution.py:24
  162.7 4.0 %multiply_convert_fusion = bf16[8,512,512]{2,1,0:T(8,128)(2,1)S(1)} fusion(f32[8,512]{1,0:T(8,128)S(1)} %copy-done.27, pred[512,512]{1,0:T(8,128)(4,1)} %iota_compare_fusion, bf16[512,8,128]{0,2,1:T(8,128)(2,1)} %bitcast.185, bf16[64,8,8,128]{3,2,1,0:T(8,128)(2,1)S(1)} %fusion.49), kind=kOutput, calls=%fused_computation.4 | convolution fusion | flops 547356672 | bytes 6569984 | tf_op jit(solution)/shard_map/nthe,nshe->nhts/dot_general | solution.py:171
  166.7 1.5 fusion.62
  169.7 1.3 copy-done.5
  171.9 1.2 copy.186
  173.1 4.4 %fusion.64 = f32[8,128,512]{2,1,0:T(8,128)} fusion(bf16[512,8,128]{0,2,1:T(8,128)(2,1)S(1)} %bitcast.187, bf16[8,512,512]{2,1,0:T(8,128)(2,1)} %copy-done.2), kind=kOutput, calls=%fused_computation.139 | convolution fusion | flops 536870912 | bytes 7340032 | tf_op jit(solution)/shard_map/nhts,nthe->nshe/dot_general | solution.py:204
  177.5 2.0 fusion.63
  179.6 13.5 %all-gather.9.cloned.1.call-done = bf16[128,128,128]{2,1,0:T(8,128)(2,1)} async-done(((bf16[8,128,128]{2,1,0:T(8,128)(2,1)}), bf16[128,128,128]{2,1,0:T(8,128)(2,1)}) %all-gather.9.cloned.1.call-update) | async-done | bytes 4194320 | tf_op jit(solution)/shard_map/all_gather | solution.py:24
  193.1 17.3 %while.9 = (s32[]{:T(128)}, f32[8,128,128]{2,1,0:T(8,128)S(1)}, s32[]{:T(128)}, bf16[16,8]{1,0:T(8,128)(2,1)S(1)}, bf16[16,8,128,128]{3,2,1,0:T(8,128)(2,1)}, /*index=5*/s32[]{:T(128)}, s32[]{:T(128)}, s32[]{:T(128)}, s32[]{:T(128)}) while((s32[]{:T(128)}, f32[8,128,128]{2,1,0:T(8,128)S(1)}, s32[]{:T(128)}, bf16[16,8]{1,0:T(8,128)(2,1)S(1)}, ...), condition=%wide.region_8.9_spmd, body=%wide.region_7.8_spmd.sunk | while | flops 393230 | bytes 1310955 | solution.py:39
  193.2 1.1 convert_add_fusion.2
  196.6 1.1 convert_add_fusion.2
  210.4 2.4 fusion.35
  212.9 1.3 copy-done.6
  214.4 2.4 fusion.36
  216.8 1.3 copy-done.7
  218.4 1.6 collective-permute-start.1
  220.0 3.0 copy.176
  222.9 2.9 copy.192
  225.9 2.9 copy.190
  228.8 8.9 %multiply_reduce_fusion.3 = (f32[1024]{0:T(1024)S(1)}, f32[1024]{0:T(1024)S(1)}, f32[1024]{0:T(1024)S(1)}, f32[1024]{0:T(1024)S(1)}, bf16[512,1024]{1,0:T(8,128)(2,1)}) fusion(f32[512,1024]{1,0:T(8,128)} %copy.192, f32[515,1024]{1,0:T(8,128)} %maximum_convert_fusion, f32[3,1024]{1,0:T(4,128)S(1)} %get-tuple-element.188, f32[1024]{0:T(1024)S(1)} %bitcast.227, ...), kind=kLoop, calls=%fused_computation.62 | loop fusion | flops 9957376 | bytes 11579392 | tf_op jit(solution)/shard_map/reduce_sum | solution.py:86
  237.7 2.9 multiply_reduce_fusion.11
  240.6 2.9 multiply_reduce_fusion.7
  243.7 59.3 %all-reduce = (f32[3,4,1024]{2,1,0:T(4,128)}, f32[1024]{0:T(1024)}) all-reduce(f32[3,4,1024]{2,1,0:T(4,128)S(1)} %pad_maximum_fusion.4, f32[1024]{0:T(1024)S(1)} %get-tuple-element.165), channel_id=1, replica_groups=mesh['ctx'=16,'head'=2] {'ctx'}, use_global_device_ids=true, to_apply=%region_21.22 | all-reduce | flops 13312 | bytes 106496 | tf_op jit(solution)/shard_map/psum | solution.py:226
  (133 shorter events, 27.2 us)
Async XLA Ops:
  7.2 9.3 %copy-start.21 = (bf16[512,1024]{1,0:T(8,128)(2,1)S(1)}, bf16[512,1024]{1,0:T(8,128)(2,1)}, u32[]{:S(2)}) copy-start(bf16[512,1024]{1,0:T(8,128)(2,1)} %param.11) | copy-start | bytes 3145732
  7.2 97.9 %all-gather.7.cloned.1.call-start = ((), (), s32[]{:S(2)}) async-start(), calls=%async_computation | async-start | bytes 8912896 | tf_op jit(solution)/shard_map/all_gather | solution.py:144
  8.8 7.1 %collective-permute-start = (bf16[3,3,1024]{2,1,0:T(4,128)(2,1)S(1)}, bf16[3,3,1024]{2,1,0:T(4,128)(2,1)S(1)}, u32[]{:S(2)}, u32[]{:S(2)}) collective-permute-start(bf16[3,3,1024]{2,1,0:T(4,128)(2,1)S(1)} %pad_maximum_fusion.5), channel_id=1, source_target_pairs={{0,2},{2,4},{4,6},{6,8},{8,10},{10,12},{12,14},{14,16},{16,18},{18... | collective-permute-start | bytes 55304 | tf_op jit(solution)/shard_map/ppermute | solution.py:16
  13.6 2.1 copy-start.24
  15.7 2.5 copy-start.22
  15.8 10.3 %copy-start.28 = (f32[8]{0:T(128)}, f32[8]{0:T(128)S(1)}, u32[]{:S(2)}) copy-start(f32[8]{0:T(128)S(1)} %exponential_multiply_fusion) | copy-start | bytes 100
  21.2 4.9 %copy-start.18 = (bf16[512,8,128]{0,2,1:T(8,128)(2,1)S(1)}, bf16[512,8,128]{0,2,1:T(8,128)(2,1)}, u32[]{:S(2)}) copy-start(bf16[512,8,128]{0,2,1:T(8,128)(2,1)} %copy.163) | copy-start | bytes 3145732
  26.1 136.6 %copy-start.8 = (bf16[64,8,8,128]{3,2,1,0:T(8,128)(2,1)}, bf16[64,8,8,128]{3,2,1,0:T(8,128)(2,1)S(1)}, u32[]{:S(2)}) copy-start(bf16[64,8,8,128]{3,2,1,0:T(8,128)(2,1)S(1)} %fusion.49) | copy-start | bytes 3145732
  27.4 165.6 %all-gather.9.cloned.1.call-start = ((), (), s32[]{:S(2)}) async-start(), calls=%async_computation.1 | async-start | bytes 4456448 | tf_op jit(solution)/shard_map/all_gather | solution.py:24
  55.2 1.3 copy-start
  60.7 1.2 copy-start.9
  60.7 1.3 copy-start.23
  60.8 1.3 copy-start.26
  61.7 3.2 %copy-start.20 = (bf16[64,8,8,128]{3,2,1,0:T(8,128)(2,1)}, bf16[64,8,8,128]{3,2,1,0:T(8,128)(2,1)S(1)}, u32[]{:S(2)}) copy-start(bf16[64,8,8,128]{3,2,1,0:T(8,128)(2,1)S(1)} %fusion.78) | copy-start | bytes 3145732
  65.0 2.0 copy-start.2
  105.1 12.5 %copy-start.10 = (bf16[512,1024]{0,1:T(8,128)(2,1)S(1)}, bf16[512,1024]{0,1:T(8,128)(2,1)}, u32[]{:S(2)}) copy-start(bf16[512,1024]{0,1:T(8,128)(2,1)} %copy.213) | copy-start | bytes 3145732
  105.1 12.5 %copy-start.13 = (f32[8,128,512]{2,1,0:T(8,128)S(1)}, f32[8,128,512]{2,1,0:T(8,128)}, u32[]{:S(2)}) copy-start(f32[8,128,512]{2,1,0:T(8,128)} %fusion.42) | copy-start | bytes 6291460
  117.6 1.9 copy-start.16
  124.7 2.9 copy-start.25
  139.0 2.3 copy-start.29
  139.0 23.6 %copy-start.27 = (f32[8,512]{1,0:T(8,128)S(1)}, f32[8,512]{1,0:T(8,128)}, u32[]{:S(2)}) copy-start(f32[8,512]{1,0:T(8,128)} %bitcast_add_fusion) | copy-start | bytes 49156
  162.7 4.1 %copy-start.19 = (bf16[512,8,128]{0,2,1:T(8,128)(2,1)S(1)}, bf16[512,8,128]{0,2,1:T(8,128)(2,1)}, u32[]{:S(2)}) copy-start(bf16[512,8,128]{0,2,1:T(8,128)(2,1)} %copy.163) | copy-start | bytes 3145732
  166.7 2.3 copy-start.3
  166.7 2.3 copy-start.12
  166.7 2.5 copy-start.17
  169.7 1.3 copy-start.5
  173.1 4.4 %copy-start.4 = (bf16[8,512,512]{2,1,0:T(8,128)(2,1)S(1)}, bf16[8,512,512]{2,1,0:T(8,128)(2,1)}, u32[]{:S(2)}) copy-start(bf16[8,512,512]{2,1,0:T(8,128)(2,1)} %copy-done.3) | copy-start | bytes 12582916
  173.1 4.4 %copy-start.11 = (bf16[512,1024]{0,1:T(8,128)(2,1)S(1)}, bf16[512,1024]{0,1:T(8,128)(2,1)}, u32[]{:S(2)}) copy-start(bf16[512,1024]{0,1:T(8,128)(2,1)} %copy.213) | copy-start | bytes 3145732
  212.9 1.3 copy-start.6
  216.8 1.3 copy-start.7
  218.4 10.3 %collective-permute-start.1 = (f32[3,3,1024]{2,1,0:T(4,128)S(1)}, f32[3,3,1024]{2,1,0:T(4,128)S(1)}, u32[]{:S(2)}, u32[]{:S(2)}) collective-permute-start(f32[3,3,1024]{2,1,0:T(4,128)S(1)} %pad_maximum_fusion.3), channel_id=1, source_target_pairs={{2,0},{4,2},{6,4},{8,6},{10,8},{12,10},{14,12},{16,14},{18,16},{20... | collective-permute-start | bytes 110600 | tf_op jit(solution)/shard_map/ppermute | solution.py:16
  228.8 8.9 %copy-start.1 = (f32[515,1024]{1,0:T(8,128)S(1)}, f32[515,1024]{1,0:T(8,128)}, u32[]{:S(2)}) copy-start(f32[515,1024]{1,0:T(8,128)} %copy-done) | copy-start | bytes 6328324
  228.8 8.9 %copy-start.15 = (f32[512,1024]{1,0:T(8,128)S(1)}, f32[512,1024]{1,0:T(8,128)}, u32[]{:S(2)}) copy-start(f32[512,1024]{1,0:T(8,128)} %copy.176) | copy-start | bytes 6291460
  237.7 3.0 copy-start.14
Sparse Core Ops, SparseCore 0:
  27.6 77.4 all-gather.6
  144.1 48.9 all-gather.8
where the time goes:
time: 311 us; the launch traced here: 310 us
  blocking collectives  111 us (36%)
  other arithmetic  55.7 us (18%)
  waiting for transfers between devices  48.9 us (16%)
  matrix products  41.3 us (13%)
  local copies, waits for them, and re-layouts  34.1 us (11%)
  between operations  14.5 us (5%)
  starting transfers between devices  3.99 us (1%)
    psum x1, blocking collectives, body(): conv_grad, gain_grad = lax.psum((conv_part, gain_part), 'ctx')  59.3 us
    all_gather x1, waiting for transfers between devices, body(): lax.all_gather(device_sum[1][None], 'ctx', axis=0, tiled=True)  35.3 us
    all_gather x1, blocking collectives, body(): all_totals = lax.all_gather(device_sum[0][None], 'ctx', axis=0, tiled=True)  22.8 us
    all_gather x1, blocking collectives, prefix(): lax.all_gather(a.astype(kind), axis)  18.6 us
    add x15, other arithmetic, chain_step(): jnp.exp(later_part[0])[..., None, None] * earlier[1] + later_part[1]  16.6 us
    reduce_sum x3, other arithmetic, conv_backward(): jnp.sum(grad_rows * extended[TAPS - 1:TAPS - 1 + tok_here], axis=0)  14.7 us
    all_gather x1, waiting for transfers between devices, prefix(): lax.all_gather(a.astype(kind), axis)  13.5 us
    dot_general x1, matrix products, body(): jnp.einsum('nh,nhde->hde', factor_table, lax.all_gather(device_sum[1][Non...  12.5 us
  transfers between devices with their start and end apart: 4, of which 2 were waited for; matrix products, arithmetic and copies ran while one was open for 14% of the time, Pallas kernels for 0%

commit v1 on v0

--- a/solution.py
+++ b/solution.py
@@ -128,7 +128,15 @@
     )
     device_sum, before = local_chain(closing, blocks, False)
     zero_state = jnp.zeros((heads_here, HD, HD), jnp.float32)
-    all_totals = lax.all_gather(device_sum[0][None], "ctx", axis=0, tiled=True)
+    ways, here = (lax.axis_size("ctx"), lax.axis_index("ctx"))
+    grown, reach = (device_sum[0][None], 1)
+    while reach < ways:
+        theirs = lax.ppermute(grown, "ctx", [(d, d ^ reach) for d in range(ways)])
+        mine_first = jnp.concatenate([grown, theirs], axis=0)
+        theirs_first = jnp.concatenate([theirs, grown], axis=0)
+        grown = jnp.where(here & reach == 0, mine_first, theirs_first)
+        reach = 2 * reach
+    all_totals = grown
     device_index = lax.axis_index("ctx")
     cumulative = jnp.cumsum(all_totals, axis=0)
     before_me = cumulative[device_index] - all_totals[device_index]

time: 311 us -> 311 us (level)
  blocking collectives: 111 us -> 88 us
  waiting for transfers between devices: 48.9 us -> 63.6 us
  starting transfers between devices: 3.99 us -> 12.7 us
    all_gather x1 -> x0, blocking collectives: 22.8 us -> none  [body(): all_totals = lax.all_gather(device_sum[0][None], 'ctx', axis=0, tiled=True)]
    all_gather x1, waiting for transfers between devices: 35.3 us -> 43.9 us  [body(): lax.all_gather(device_sum[1][None], 'ctx', axis=0, tiled=True)]
    ppermute x0 -> x4, starting transfers between devices: none -> 8.51 us  [body(): theirs = lax.ppermute(grown, 'ctx', [(d, d ^ reach) for d in range(ways)])]
    ppermute x0 -> x4, waiting for transfers between devices: none -> 6.11 us  [body(): theirs = lax.ppermute(grown, 'ctx', [(d, d ^ reach) for d in range(ways)])]
    unnamed x3 -> x4, other arithmetic: 6.81 us -> 7.4 us
    another operation x8 -> x5, local copies, waits for them, and re-layouts: 6.37 us -> 6.04 us
    unnamed x61 -> x55, local copies, waits for them, and re-layouts: 8.88 us -> 8.84 us
  transfers between devices with their start and end apart: 4 -> 8, of which waited for: 2 -> 5; matrix products, arithmetic and copies ran while one was open for 14% -> 14% of each run, Pallas kernels for 0% -> 0%
where the time goes in v1:
time: 311 us; the launch traced here: 310 us
  blocking collectives  88 us (28%)
  waiting for transfers between devices  63.6 us (20%)
  other arithmetic  57.5 us (18%)
  matrix products  41.3 us (13%)
  local copies, waits for them, and re-layouts  32.1 us (10%)
  between operations  14.5 us (5%)
  starting transfers between devices  12.7 us (4%)
    psum x1, blocking collectives, body(): conv_grad, gain_grad = lax.psum((conv_part, gain_part), 'ctx')  59.3 us
    all_gather x1, waiting for transfers between devices, body(): lax.all_gather(device_sum[1][None], 'ctx', axis=0, tiled=True)  43.9 us
    all_gather x1, blocking collectives, prefix(): lax.all_gather(a.astype(kind), axis)  18.6 us
    add x15, other arithmetic, chain_step(): jnp.exp(later_part[0])[..., None, None] * earlier[1] + later_part[1]  16.6 us
    reduce_sum x3, other arithmetic, conv_backward(): jnp.sum(grad_rows * extended[TAPS - 1:TAPS - 1 + tok_here], axis=0)  14.7 us
    all_gather x1, waiting for transfers between devices, prefix(): lax.all_gather(a.astype(kind), axis)  13.6 us
    dot_general x1, matrix products, body(): jnp.einsum('nh,nhde->hde', factor_table, lax.all_gather(device_sum[1][Non...  12.5 us
    unnamed x55, local copies, waits for them, and re-layouts  8.84 us
  transfers between devices with their start and end apart: 8, of which 5 were waited for; matrix products, arithmetic and copies ran while one was open for 14% of the time, Pallas kernels for 0%

profile of v1, /device:TPU:0, one launch (start us, length us, event | category | flops | bytes accessed | tf_op | source)
XLA Modules:
  0.0 310.1 jit_solution(12968005588582216412)
XLA Ops:
  8.8 2.4 collective-permute-start
  11.2 2.2 reduce-window.6
  15.6 2.9 maximum_convert_fusion
  20.0 1.5 copy.153
  21.5 4.9 %fusion.49 = bf16[64,8,8,128]{3,2,1,0:T(8,128)(2,1)S(1)} fusion(f32[515,1024]{1,0:T(8,128)} %maximum_convert_fusion, f32[1024]{0:T(1024)S(1)} %bitcast.220, f32[1024]{0:T(1024)S(1)} %bitcast.222, f32[1024]{0:T(1024)S(1)} %bitcast.224, f32[1024]{0:T(1024)S(1)} %bitcast.218), kind=kLoop, calls=%fused_computation.94 | loop fusion | flops 4194304 | bytes 9453568
  28.0 2.7 collective-permute-start.1
  32.7 1.6 collective-permute-start.2
  34.2 2.0 collective-permute-done.2
  36.3 1.6 collective-permute-start.3
  37.9 2.0 collective-permute-done.3
  40.0 2.6 collective-permute-start.4
  42.6 2.1 collective-permute-done.4
  45.5 1.5 maximum_convert_fusion.1
  47.0 1.3 copy-done
  48.4 1.9 add_convert_fusion.1
  50.3 2.3 copy.200
  53.8 2.9 multiply_convert_fusion.1
  56.7 2.0 copy-done.2
  58.7 2.8 fusion.42
  61.5 43.9 %all-gather.6.cloned.1.call-done = f32[128,128,128]{2,1,0:T(8,128)} async-done(((f32[8,128,128]{2,1,0:T(8,128)}), f32[128,128,128]{2,1,0:T(8,128)}) %all-gather.6.cloned.1.call-update) | async-done | bytes 8388624 | tf_op jit(solution)/shard_map/all_gather | solution.py:152
  105.4 12.5 %fusion = f32[8,1,128,128]{3,1,2,0:T(1,128)S(1)} fusion(f32[16,8,1,1]{0,2,3,1:T(1,128)S(1)} %copy.194, f32[16,8,128,128]{3,2,1,0:T(8,128)} %bitcast.189), kind=kOutput, calls=%fused_computation.2 | convolution fusion | flops 25165824 | bytes 8913408 | tf_op jit(solution)/shard_map/nh,nhde->hde/dot_general | solution.py:149
  118.0 1.9 multiply_reduce_fusion.12
  119.8 5.1 %psum.28 = f32[512]{0:T(512)S(1)} all-reduce(f32[512]{0:T(512)S(1)} %get-tuple-element.206), channel_id=1, replica_groups=mesh['ctx'=16,'head'=2] {'head'}, use_global_device_ids=true, to_apply=%region_4.5 | all-reduce | flops 512 | bytes 4096 | tf_op jit(solution)/shard_map/psum | solution.py:168
  125.0 2.9 copy.157
  127.9 2.6 fusion.7
  130.5 4.9 %psum.29 = f32[512]{0:T(512)S(1)} all-reduce(f32[512]{0:T(512)S(1)} %get-tuple-element.166), channel_id=1, replica_groups=mesh['ctx'=16,'head'=2] {'head'}, use_global_device_ids=true, to_apply=%region_6.7 | all-reduce | flops 512 | bytes 4096 | tf_op jit(solution)/shard_map/psum | solution.py:170
  135.5 3.9 %fusion.6 = (bf16[512,1024]{1,0:T(8,128)(2,1)}, bf16[512,1024]{1,0:T(8,128)(2,1)}) fusion(bf16[512,1024]{1,0:T(8,128)(2,1)} %param.15, f32[512,1024]{1,0:T(8,128)} %copy.157, f32[512]{0:T(512)S(1)} %multiply_multiply_fusion, f32[1024]{0:T(1024)S(1)} %copy-done.22, f32[512]{0:T(512)S(1)} %add_rsqrt_fusion), kind=kLoop, calls=%fused_computation.19 | loop fusion | flops 4718592 | bytes 5251072 | tf_op jit(solution)/shard_map/convert_element_type | solution.py:43
  139.3 2.3 copy.201
  141.6 2.7 fusion.39
  144.3 18.6 %all-gather.2 = bf16[16,1,8]{2,1,0:T(2,128)(2,1)S(1)} all-gather(bf16[1,1,8]{2,1,0:T(2,128)(2,1)S(1)} %copy-done.24), channel_id=1, replica_groups=mesh['ctx'=16,'head'=2] {'ctx'}, dimensions={0}, use_global_device_ids=true | all-gather | bytes 272 | tf_op jit(solution)/shard_map/all_gather | solution.py:24
  163.0 4.0 %multiply_convert_fusion = bf16[8,512,512]{2,1,0:T(8,128)(2,1)S(1)} fusion(f32[8,512]{1,0:T(8,128)} %bitcast_add_fusion.1, pred[512,512]{1,0:T(8,128)(4,1)S(1)} %iota_compare_fusion, bf16[512,8,128]{0,2,1:T(8,128)(2,1)} %bitcast.186, bf16[64,8,8,128]{3,2,1,0:T(8,128)(2,1)S(1)} %fusion.49), kind=kOutput, calls=%fused_computation.4 | convolution fusion | flops 547356672 | bytes 6569984 | tf_op jit(solution)/shard_map/nthe,nshe->nhts/dot_general | solution.py:179
  167.0 1.5 fusion.61
  170.0 1.3 copy-done.5
  173.4 4.4 %fusion.63 = f32[8,128,512]{2,1,0:T(8,128)} fusion(bf16[512,8,128]{0,2,1:T(8,128)(2,1)S(1)} %bitcast.188, bf16[8,512,512]{2,1,0:T(8,128)(2,1)} %copy-done.2), kind=kOutput, calls=%fused_computation.142 | convolution fusion | flops 536870912 | bytes 7340032 | tf_op jit(solution)/shard_map/nhts,nthe->nshe/dot_general | solution.py:212
  177.8 2.0 fusion.62
  179.8 13.6 %all-gather.8.cloned.1.call-done = bf16[128,128,128]{2,1,0:T(8,128)(2,1)} async-done(((bf16[8,128,128]{2,1,0:T(8,128)(2,1)}), bf16[128,128,128]{2,1,0:T(8,128)(2,1)}) %all-gather.8.cloned.1.call-update) | async-done | bytes 4194320 | tf_op jit(solution)/shard_map/all_gather | solution.py:24
  193.4 17.3 %while.9 = (s32[]{:T(128)}, f32[8,128,128]{2,1,0:T(8,128)S(1)}, s32[]{:T(128)}, bf16[16,8]{1,0:T(8,128)(2,1)S(1)}, bf16[16,8,128,128]{3,2,1,0:T(8,128)(2,1)}, /*index=5*/s32[]{:T(128)}, s32[]{:T(128)}, s32[]{:T(128)}, s32[]{:T(128)}) while((s32[]{:T(128)}, f32[8,128,128]{2,1,0:T(8,128)S(1)}, s32[]{:T(128)}, bf16[16,8]{1,0:T(8,128)(2,1)S(1)}, ...), condition=%wide.region_8.9_spmd, body=%wide.region_7.8_spmd.sunk | while | flops 393230 | bytes 1310955 | solution.py:39
  210.7 2.4 fusion.35
  214.7 2.4 fusion.36
  217.1 1.3 copy-done.7
  218.7 1.6 collective-permute-start.5
  220.3 3.0 copy.164
  223.2 2.9 copy.180
  226.1 2.9 copy.178
  229.1 8.9 %multiply_reduce_fusion.3 = (f32[1024]{0:T(1024)S(1)}, f32[1024]{0:T(1024)S(1)}, f32[1024]{0:T(1024)S(1)}, f32[1024]{0:T(1024)S(1)}, bf16[512,1024]{1,0:T(8,128)(2,1)}) fusion(f32[512,1024]{1,0:T(8,128)} %copy.180, f32[515,1024]{1,0:T(8,128)} %maximum_convert_fusion, f32[3,1024]{1,0:T(4,128)S(1)} %get-tuple-element.186, f32[1024]{0:T(1024)S(1)} %bitcast.221, ...), kind=kLoop, calls=%fused_computation.62 | loop fusion | flops 9957376 | bytes 11579392 | tf_op jit(solution)/shard_map/reduce_sum | solution.py:86
  238.0 2.9 multiply_reduce_fusion.11
  240.9 2.9 multiply_reduce_fusion.7
  243.9 59.3 %all-reduce = (f32[3,4,1024]{2,1,0:T(4,128)}, f32[1024]{0:T(1024)}) all-reduce(f32[3,4,1024]{2,1,0:T(4,128)S(1)} %pad_maximum_fusion.4, f32[1024]{0:T(1024)S(1)} %get-tuple-element.165), channel_id=1, replica_groups=mesh['ctx'=16,'head'=2] {'ctx'}, use_global_device_ids=true, to_apply=%region_21.22 | all-reduce | flops 13312 | bytes 106496 | tf_op jit(solution)/shard_map/psum | solution.py:234
  (132 shorter events, 33.4 us)
Async XLA Ops:
  7.2 11.3 %copy-start.21 = (bf16[512,1024]{1,0:T(8,128)(2,1)S(1)}, bf16[512,1024]{1,0:T(8,128)(2,1)}, u32[]{:S(2)}) copy-start(bf16[512,1024]{1,0:T(8,128)(2,1)} %param.10) | copy-start | bytes 3145732
  7.2 98.3 %all-gather.6.cloned.1.call-start = ((), (), s32[]{:S(2)}) async-start(), calls=%async_computation | async-start | bytes 8912896 | tf_op jit(solution)/shard_map/all_gather | solution.py:152
  8.8 6.7 %collective-permute-start = (bf16[3,3,1024]{2,1,0:T(4,128)(2,1)S(1)}, bf16[3,3,1024]{2,1,0:T(4,128)(2,1)S(1)}, u32[]{:S(2)}, u32[]{:S(2)}) collective-permute-start(bf16[3,3,1024]{2,1,0:T(4,128)(2,1)S(1)} %pad_maximum_fusion.5), channel_id=1, source_target_pairs={{0,2},{2,4},{4,6},{6,8},{8,10},{10,12},{12,14},{14,16},{16,18},{18... | collective-permute-start | bytes 55304 | tf_op jit(solution)/shard_map/ppermute | solution.py:16
  15.5 10.9 %copy-start.25 = (f32[8]{0:T(128)}, f32[8]{0:T(128)S(1)}, u32[]{:S(2)}) copy-start(f32[8]{0:T(128)S(1)} %get-tuple-element.205) | copy-start | bytes 100
  21.5 4.9 %copy-start.18 = (bf16[512,8,128]{0,2,1:T(8,128)(2,1)S(1)}, bf16[512,8,128]{0,2,1:T(8,128)(2,1)}, u32[]{:S(2)}) copy-start(bf16[512,8,128]{0,2,1:T(8,128)(2,1)} %copy.153) | copy-start | bytes 3145732
  26.4 136.6 %copy-start.8 = (bf16[64,8,8,128]{3,2,1,0:T(8,128)(2,1)}, bf16[64,8,8,128]{3,2,1,0:T(8,128)(2,1)S(1)}, u32[]{:S(2)}) copy-start(bf16[64,8,8,128]{3,2,1,0:T(8,128)(2,1)S(1)} %fusion.49) | copy-start | bytes 3145732
  27.7 165.6 %all-gather.8.cloned.1.call-start = ((), (), s32[]{:S(2)}) async-start(), calls=%async_computation.1 | async-start | bytes 4456448 | tf_op jit(solution)/shard_map/all_gather | solution.py:24
  28.0 3.9 %collective-permute-start.1 = (f32[1,8]{1,0:T(1,128)S(1)}, f32[1,8]{1,0:T(1,128)}, u32[]{:S(2)}, u32[]{:S(2)}) collective-permute-start(f32[1,8]{1,0:T(1,128)S(1)} %bitcast.240), channel_id=1, source_target_pairs={{0,2},{2,0},{4,6},{6,4},{8,10},{10,8},{12,14},{14,12},{16,18},{18,... | collective-permute-start | bytes 104 | tf_op jit(solution)/shard_map/ppermute | solution.py:134
  32.7 3.6 %collective-permute-start.2 = (f32[2,8]{1,0:T(2,128)S(1)}, f32[2,8]{1,0:T(2,128)S(1)}, u32[]{:S(2)}, u32[]{:S(2)}) collective-permute-start(f32[2,8]{1,0:T(2,128)S(1)} %maximum_select_fusion.3), channel_id=1, source_target_pairs={{0,4},{2,6},{4,0},{6,2},{8,12},{10,14},{12,8},{14,10},{16,20},{18,... | collective-permute-start | bytes 200 | tf_op jit(solution)/shard_map/ppermute | solution.py:134
  36.3 3.7 %collective-permute-start.3 = (f32[4,8]{1,0:T(4,128)S(1)}, f32[4,8]{1,0:T(4,128)S(1)}, u32[]{:S(2)}, u32[]{:S(2)}) collective-permute-start(f32[4,8]{1,0:T(4,128)S(1)} %maximum_select_fusion.2), channel_id=1, source_target_pairs={{0,8},{2,10},{4,12},{6,14},{8,0},{10,2},{12,4},{14,6},{16,24},{18,... | collective-permute-start | bytes 392 | tf_op jit(solution)/shard_map/ppermute | solution.py:134
  40.0 4.7 %collective-permute-start.4 = (f32[8,8]{1,0:T(8,128)S(1)}, f32[8,8]{1,0:T(8,128)S(1)}, u32[]{:S(2)}, u32[]{:S(2)}) collective-permute-start(f32[8,8]{1,0:T(8,128)S(1)} %maximum_select_fusion.1), channel_id=1, source_target_pairs={{0,16},{2,18},{4,20},{6,22},{8,24},{10,26},{12,28},{14,30},{16,0},... | collective-permute-start | bytes 776 | tf_op jit(solution)/shard_map/ppermute | solution.py:134
  47.0 1.3 copy-start
  52.5 1.2 copy-start.9
  52.5 1.2 copy-start.23
  53.5 3.2 %copy-start.20 = (bf16[64,8,8,128]{3,2,1,0:T(8,128)(2,1)}, bf16[64,8,8,128]{3,2,1,0:T(8,128)(2,1)S(1)}, u32[]{:S(2)}) copy-start(bf16[64,8,8,128]{3,2,1,0:T(8,128)(2,1)S(1)} %fusion.77) | copy-start | bytes 3145732
  56.7 2.0 copy-start.2
  105.4 12.5 %copy-start.10 = (bf16[512,1024]{0,1:T(8,128)(2,1)S(1)}, bf16[512,1024]{0,1:T(8,128)(2,1)}, u32[]{:S(2)}) copy-start(bf16[512,1024]{0,1:T(8,128)(2,1)} %copy.200) | copy-start | bytes 3145732
  105.4 12.5 %copy-start.13 = (f32[8,128,512]{2,1,0:T(8,128)S(1)}, f32[8,128,512]{2,1,0:T(8,128)}, u32[]{:S(2)}) copy-start(f32[8,128,512]{2,1,0:T(8,128)} %fusion.42) | copy-start | bytes 6291460
  117.9 1.9 copy-start.16
  125.0 2.9 copy-start.22
  139.3 2.3 copy-start.26
  139.3 5.0 %copy-start.24 = (bf16[1,1,8]{2,1,0:T(2,128)(2,1)S(1)}, bf16[1,1,8]{2,1,0:T(2,128)(2,1)}, u32[]{:S(2)}) copy-start(bf16[1,1,8]{2,1,0:T(2,128)(2,1)} %get-tuple-element.204) | copy-start | bytes 52
  163.0 4.0 %copy-start.19 = (bf16[512,8,128]{0,2,1:T(8,128)(2,1)S(1)}, bf16[512,8,128]{0,2,1:T(8,128)(2,1)}, u32[]{:S(2)}) copy-start(bf16[512,8,128]{0,2,1:T(8,128)(2,1)} %copy.153) | copy-start | bytes 3145732
  167.0 2.3 copy-start.3
  167.0 2.3 copy-start.12
  167.0 2.5 copy-start.17
  170.0 1.3 copy-start.5
  173.4 4.4 %copy-start.4 = (bf16[8,512,512]{2,1,0:T(8,128)(2,1)S(1)}, bf16[8,512,512]{2,1,0:T(8,128)(2,1)}, u32[]{:S(2)}) copy-start(bf16[8,512,512]{2,1,0:T(8,128)(2,1)} %copy-done.3) | copy-start | bytes 12582916
  173.4 4.4 %copy-start.11 = (bf16[512,1024]{0,1:T(8,128)(2,1)S(1)}, bf16[512,1024]{0,1:T(8,128)(2,1)}, u32[]{:S(2)}) copy-start(bf16[512,1024]{0,1:T(8,128)(2,1)} %copy.200) | copy-start | bytes 3145732
  213.2 1.3 copy-start.6
  217.1 1.3 copy-start.7
  218.7 10.3 %collective-permute-start.5 = (f32[3,3,1024]{2,1,0:T(4,128)S(1)}, f32[3,3,1024]{2,1,0:T(4,128)S(1)}, u32[]{:S(2)}, u32[]{:S(2)}) collective-permute-start(f32[3,3,1024]{2,1,0:T(4,128)S(1)} %pad_maximum_fusion.3), channel_id=1, source_target_pairs={{2,0},{4,2},{6,4},{8,6},{10,8},{12,10},{14,12},{16,14},{18,16},{20... | collective-permute-start | bytes 110600 | tf_op jit(solution)/shard_map/ppermute | solution.py:16
  229.0 8.9 %copy-start.1 = (f32[515,1024]{1,0:T(8,128)S(1)}, f32[515,1024]{1,0:T(8,128)}, u32[]{:S(2)}) copy-start(f32[515,1024]{1,0:T(8,128)} %copy-done) | copy-start | bytes 6328324
  229.1 8.9 %copy-start.15 = (f32[512,1024]{1,0:T(8,128)S(1)}, f32[512,1024]{1,0:T(8,128)}, u32[]{:S(2)}) copy-start(f32[512,1024]{1,0:T(8,128)} %copy.164) | copy-start | bytes 6291460
  238.0 3.0 copy-start.14
Sparse Core Ops, SparseCore 0:
  27.9 77.5 all-gather.5
  144.4 48.9 all-gather.7
